TPU v7x, 32 devices: a whole 2x2x4 slice. The times are simulated.
32 devices in a mesh: row: 8 (over z, core), col: 4 (over y, x).
Axes of the slice: x: 2, y: 2, z: 4, core: 2. Of those that a mesh axis runs over, the one named last changes fastest.
Arguments:
- coeffs: bfloat16 [256, 64, 128], P(('row', 'col')), may hold values from -6 to 6
- blocks: bfloat16 [16384, 64, 64], P(('row', 'col')), may hold values from -0.046875 to 0.046875
- blk_rows: int32 [16384], P(('row', 'col')), may hold values from 0 to 255, as said below
- blk_cols: int32 [16384], P(('row', 'col')), may hold values from 0 to 255, as said below
- blk_count: int32 [32], P(('row', 'col')), may hold values from 0 to 512, as said below
Outputs:
- product: float32 [256, 64, 128], P(('row', 'col'))
Inputs may be any that keep to these rules, and one draw needn't show every extreme that they name: `blk_rows`: element e belongs to device e // 8 in row+col order. In the first blk_count slots of a device, I <= J, I belongs to a device of the same row index, and J to a device of the same column index whose row index exceeds that of I's device by 0 to 3; the difference 3 occurs in every draw. Later slots hold elements of the device's own row and column groups and are unused; pairs may repeat. `blk_cols`: see blk_rows. `blk_count`: counts differ widely between devices; some device uses all 512 slots in every draw.
All inputs are finite; a program needn't handle non-finite values.
Results may differ from a plain program's by a relative error of at most 0.0003.
Values may be sent and summed in bfloat16 or wider, within the bound.
No kernel may reach another device: no remote copies, remote signals or barrier semaphores. Data moves between devices by JAX's collectives and lax.ppermute only.
A program may use at most 128 MiB of HBM per device.

v0:
```python
import jax
import jax.numpy as jnp
from jax import lax
from jax.sharding import PartitionSpec as P

REACH = 3


def from_behind(block, axis, distance):
    devices = range(lax.axis_size(axis))
    route = [(i - distance, i) for i in devices if i - distance in devices]
    return lax.ppermute(block, axis, route)


def body(coeffs, blocks, blk_rows, blk_cols, blk_count):
    high_precision = lax.Precision.HIGHEST
    elem_dev, width, sides = coeffs.shape
    slot_total = blocks.shape[0]
    my_row = lax.axis_index("row")
    segment = elem_dev * lax.axis_size("col")
    window = (REACH + 1) * elem_dev
    row_group = lax.all_gather(coeffs, "col", axis=0, tiled=True)
    gathered = coeffs
    spread = 1
    for level in range(REACH.bit_length()):
        arrived = from_behind(gathered, "row", -spread)
        gathered = jnp.concatenate([gathered, arrived], axis=0)
        spread = spread * 2
    active = jnp.arange(slot_total, dtype=jnp.int32) < blk_count[0]
    mirror = active & (blk_rows != blk_cols)
    row_local = jnp.clip(blk_rows - my_row * segment, 0, segment - 1)
    col_local = (blk_cols // segment - my_row) * elem_dev + blk_cols % elem_dev
    col_local = jnp.clip(col_local, 0, window - 1)
    column_entries = gathered[col_local]
    row_contributions = jnp.einsum(
        "gjc,gcx->gjx", blocks, column_entries, preferred_element_type=jnp.float32
    )
    row_contributions = row_contributions.reshape(slot_total, width * sides)
    row_select = (
        (row_local[None, :] == jnp.arange(segment, dtype=jnp.int32)[:, None]) & active[None, :]
    ).astype(jnp.float32)
    row_entries = row_group[row_local]
    column_contributions = jnp.einsum(
        "ihv,ihe->ive", blocks, row_entries, preferred_element_type=jnp.float32
    )
    column_contributions = column_contributions.reshape(slot_total, width * sides)
    col_select = (
        (col_local[None, :] == jnp.arange(window, dtype=jnp.int32)[:, None]) & mirror[None, :]
    ).astype(jnp.float32)
    col_part = jnp.dot(
        col_select,
        column_contributions,
        precision=high_precision,
        preferred_element_type=jnp.float32,
    )
    row_part = jnp.dot(
        row_select, row_contributions, precision=high_precision, preferred_element_type=jnp.float32
    )
    row_sums = lax.psum_scatter(row_part, "col", scatter_dimension=0, tiled=True)
    col_sums = col_part[:elem_dev]
    for offset in range(1, REACH + 1):
        piece = col_part[offset * elem_dev : (offset + 1) * elem_dev]
        col_sums = col_sums + from_behind(piece, "row", offset)
    return (row_sums + col_sums).reshape(elem_dev, width, sides)


def solution(mesh):
    placed = (
        P(("row", "col"), None, None),
        P(("row", "col"), None, None),
        P(("row", "col")),
        P(("row", "col")),
        P(("row", "col")),
    )
    return jax.shard_map(
        body, mesh=mesh, in_specs=placed, out_specs=P(("row", "col"), None, None), check_vma=False
    )
```

profile of v0, /device:TPU:0, one launch (start us, length us, event | category | flops | bytes accessed | tf_op | source)
XLA Modules:
  0.0 199.8 jit_solution(3817646635028299067)
XLA Ops:
  6.5 0.0 copy-start.2
  6.5 0.0 all-reduce.3.cloned.1.call-start
  6.5 1.4 collective-permute-start
  8.0 13.1 %all_gather.3 = bf16[32,64,128]{2,1,0:T(8,128)(2,1)S(1)} all-gather(bf16[8,64,128]{2,1,0:T(8,128)(2,1)} %param.5), channel_id=1, replica_groups=mesh['row'=8,'col'=4] {'col'}, dimensions={0}, use_global_device_ids=true | all-gather | bytes 655360 | tf_op jit(solution)/shard_map/all_gather | solution.py:22
  21.1 0.7 compare_select_fusion
  21.8 15.7 %copy.10 = bf16[512,64,64]{1,2,0:T(8,128)(2,1)} copy(bf16[512,64,64]{0,2,1:T(8,128)(2,1)} %param.6) | data formatting | bytes 8388608 | tf_op args[1]
  37.4 0.0 copy-done.2
  38.1 13.4 %gather_fusion.1 = bf16[512,64,128]{2,1,0:T(8,128)(2,1)} fusion(bf16[32,64,128]{2,1,0:T(8,128)(2,1)S(1)} %all_gather.3, s32[1024]{0:T(1024)S(1)} %pad_clamp_fusion), kind=kCustom, calls=%fused_computation.1 | custom fusion | bytes 16779264 | tf_op jit(solution)/shard_map/gather | solution.py:42
  51.5 13.9 %fusion.28 = f32[512,128,64]{1,2,0:T(8,128)} fusion(bf16[512,64,64]{1,2,0:T(8,128)(2,1)} %copy.10, bf16[512,64,128]{2,1,0:T(8,128)(2,1)} %gather_fusion.1), kind=kOutput, calls=%fused_computation.46 | convolution fusion | flops 536870912 | bytes 29360128 | tf_op jit(solution)/shard_map/ihv,ihe->ive/dot_general | solution.py:43
  65.4 0.0 copy-done.1
  65.4 0.0 collective-permute-done
  65.4 0.0 copy-done
  65.5 1.5 collective-permute-start.1
  66.9 20.3 %fusion = f32[32,8192]{1,0:T(8,128)S(1)} fusion(f32[64,8,64,128]{3,2,1,0:T(8,128)} %bitcast.20, s32[512]{0:T(512)S(1)} %get-tuple-element.6, pred[512]{0:T(512)(128)(4,1)S(1)} %compare_and_fusion), kind=kOutput, calls=%fused_computation.2 | convolution fusion | flops 1610645504 | bytes 17828352 | tf_op jit(solution)/shard_map/dot_general | solution.py:50
  87.3 0.0 collective-permute-done.1
  87.3 0.1 pad_maximum_fusion
  87.4 13.6 %gather_fusion = bf16[512,64,128]{2,1,0:T(8,128)(2,1)} fusion(bf16[32,64,128]{2,1,0:T(8,128)(2,1)S(1)} %pad_maximum_fusion, s32[1024]{0:T(1024)S(1)} %pad_clamp_fusion.1), kind=kCustom, calls=%fused_computation | custom fusion | bytes 16779264 | tf_op jit(solution)/shard_map/gather | solution.py:34
  101.0 14.4 %fusion.27 = f32[512,128,64]{1,2,0:T(8,128)} fusion(bf16[512,64,64]{1,2,0:T(8,128)(2,1)} %copy.10, bf16[512,64,128]{2,1,0:T(8,128)(2,1)} %gather_fusion), kind=kOutput, calls=%fused_computation.45 | convolution fusion | flops 536870912 | bytes 29360128 | tf_op jit(solution)/shard_map/gjc,gcx->gjx/dot_general | solution.py:35
  115.4 21.2 %fusion.3 = f32[32,8192]{1,0:T(8,128)} fusion(f32[64,8,64,128]{3,2,1,0:T(8,128)} %bitcast.21, s32[512]{0:T(512)S(1)} %get-tuple-element.8, pred[512]{0:T(512)(128)(4,1)S(1)} %iota_compare_fusion.2), kind=kOutput, calls=%fused_computation.5 | convolution fusion | flops 1610645504 | bytes 17828352 | tf_op jit(solution)/shard_map/dot_general | solution.py:56
  136.6 0.0 all-reduce.3.cloned.1.call-update
  136.6 0.1 fusion.26
  136.7 1.6 collective-permute-start.2
  138.3 5.0 %collective-permute-start.3 = (f32[8,8192]{1,0:T(8,128)S(1)}, f32[8,8192]{1,0:T(8,128)S(1)}, u32[]{:S(2)}, u32[]{:S(2)}) collective-permute-start(f32[8,8192]{1,0:T(8,128)S(1)} %get-tuple-element.11), channel_id=1, source_target_pairs={{0,8},{4,12},{8,16},{12,20},{16,24},{20,28},{1,9},{5,13},{9,17},{1... | collective-permute-start | bytes 786440 | tf_op jit(solution)/shard_map/ppermute | solution.py:12
  143.3 4.9 %collective-permute-start.4 = (f32[8,8192]{1,0:T(8,128)S(1)}, f32[8,8192]{1,0:T(8,128)S(1)}, u32[]{:S(2)}, u32[]{:S(2)}) collective-permute-start(f32[8,8192]{1,0:T(8,128)S(1)} %get-tuple-element.10), channel_id=1, source_target_pairs={{0,12},{4,16},{8,20},{12,24},{16,28},{1,13},{5,17},{9,21},{13,25},... | collective-permute-start | bytes 786440 | tf_op jit(solution)/shard_map/ppermute | solution.py:12
  148.2 0.0 copy-done.3
  148.2 0.6 dynamic-slice
  149.5 0.0 collective-permute-done.2
  149.5 0.0 collective-permute-done.3
  149.5 5.6 %collective-permute-done.4 = f32[8,8192]{1,0:T(8,128)S(1)} collective-permute-done((f32[8,8192]{1,0:T(8,128)S(1)}, f32[8,8192]{1,0:T(8,128)S(1)}, u32[]{:S(2)}, u32[]{:S(2)}) %collective-permute-start.4) | collective-permute-done | bytes 262176 | tf_op jit(solution)/shard_map/ppermute | solution.py:12
  155.1 36.1 %all-reduce.3.cloned.1.call-done = f32[32,8192]{1,0:T(8,128)} async-done(((f32[32,8192]{1,0:T(8,128)}), f32[32,8192]{1,0:T(8,128)}) %all-reduce.3.cloned.1.call-update) | async-done | bytes 1048592
  191.1 1.0 fusion.9
  192.2 0.8 copy.11
  (9 shorter events, 0.1 us)
Async XLA Ops:
  6.5 30.9 %copy-start.2 = (s32[512]{0:T(512)S(1)}, s32[512]{0:T(512)}, u32[]{:S(2)}) copy-start(s32[512]{0:T(512)} %param.8) | copy-start | bytes 6148
  6.5 184.6 %all-reduce.3.cloned.1.call-start = ((), (), s32[]{:S(2)}) async-start(), calls=%async_computation | async-start | bytes 2097152
  6.5 58.9 %collective-permute-start = (bf16[8,64,128]{2,1,0:T(8,128)(2,1)}, bf16[8,64,128]{2,1,0:T(8,128)(2,1)S(1)}, u32[]{:S(2)}, u32[]{:S(2)}) collective-permute-start(bf16[8,64,128]{2,1,0:T(8,128)(2,1)} %param.5), channel_id=1, source_target_pairs={{4,0},{8,4},{12,8},{16,12},{20,16},{24,20},{28,24},{5,1},{9,5},{13... | collective-permute-start | bytes 393224 | tf_op jit(solution)/shard_map/ppermute | solution.py:12
  51.5 13.9 %copy-start.1 = (s32[512]{0:T(512)S(1)}, s32[512]{0:T(512)}, u32[]{:S(2)}) copy-start(s32[512]{0:T(512)} %param.7) | copy-start | bytes 6148
  51.5 13.9 %copy-start = (bf16[8,64,128]{2,1,0:T(8,128)(2,1)S(1)}, bf16[8,64,128]{2,1,0:T(8,128)(2,1)}, u32[]{:S(2)}) copy-start(bf16[8,64,128]{2,1,0:T(8,128)(2,1)} %param.5) | copy-start | bytes 393220
  65.5 21.9 %collective-permute-start.1 = (bf16[16,64,128]{2,1,0:T(8,128)(2,1)S(1)}, bf16[16,64,128]{2,1,0:T(8,128)(2,1)S(1)}, u32[]{:S(2)}, u32[]{:S(2)}) collective-permute-start(bf16[16,64,128]{2,1,0:T(8,128)(2,1)S(1)} %pad_maximum_fusion.1), channel_id=1, source_target_pairs={{8,0},{12,4},{16,8},{20,12},{24,16},{28,20},{9,1},{13,5},{17,9},{2... | collective-permute-start | bytes 786440 | tf_op jit(solution)/shard_map/ppermute | solution.py:12
  115.4 32.8 %copy-start.3 = (u32[32]{0:T(128)S(1)}, u32[32]{0:T(128)}, u32[]{:S(2)}) copy-start(u32[32]{0:T(128)} %constant.46) | copy-start | bytes 388
  136.7 12.8 %collective-permute-start.2 = (f32[8,8192]{1,0:T(8,128)S(1)}, f32[8,8192]{1,0:T(8,128)S(1)}, u32[]{:S(2)}, u32[]{:S(2)}) collective-permute-start(f32[8,8192]{1,0:T(8,128)S(1)} %get-tuple-element.9), channel_id=1, source_target_pairs={{0,4},{4,8},{8,12},{12,16},{16,20},{20,24},{24,28},{1,5},{5,9},{9,... | collective-permute-start | bytes 786440 | tf_op jit(solution)/shard_map/ppermute | solution.py:12
  138.3 11.2 %collective-permute-start.3 = (f32[8,8192]{1,0:T(8,128)S(1)}, f32[8,8192]{1,0:T(8,128)S(1)}, u32[]{:S(2)}, u32[]{:S(2)}) collective-permute-start(f32[8,8192]{1,0:T(8,128)S(1)} %get-tuple-element.11), channel_id=1, source_target_pairs={{0,8},{4,12},{8,16},{12,20},{16,24},{20,28},{1,9},{5,13},{9,17},{1... | collective-permute-start | bytes 786440 | tf_op jit(solution)/shard_map/ppermute | solution.py:12
  143.3 11.8 %collective-permute-start.4 = (f32[8,8192]{1,0:T(8,128)S(1)}, f32[8,8192]{1,0:T(8,128)S(1)}, u32[]{:S(2)}, u32[]{:S(2)}) collective-permute-start(f32[8,8192]{1,0:T(8,128)S(1)} %get-tuple-element.10), channel_id=1, source_target_pairs={{0,12},{4,16},{8,20},{12,24},{16,28},{1,13},{5,17},{9,21},{13,25},... | collective-permute-start | bytes 786440 | tf_op jit(solution)/shard_map/ppermute | solution.py:12
Sparse Core Ops, SparseCore 0:
  136.8 54.3 all-reduce.2
where the time goes:
time: 200 us
  matrix products  69.8 us (35%)
  local copies, waits for them, and re-layouts  44.1 us (22%)
  waiting for transfers between devices  41.7 us (21%)
  between operations  14.8 us (7%)
  starting transfers between devices  14.4 us (7%)
  blocking collectives  13.1 us (7%)
    unnamed x2, waiting for transfers between devices  36.1 us
    dot_general x1, matrix products, body(): jnp.dot(row_select, row_contributions, precision=high_precision, preferre...  21.2 us
    dot_general x1, matrix products, body(): jnp.dot(col_select, column_contributions, precision=high_precision, prefe...  20.3 us
    unnamed x10, local copies, waits for them, and re-layouts  16.3 us
    dot_general x1, matrix products, body(): jnp.einsum('gjc,gcx->gjx', blocks, column_entries, preferred_element_type...  14.4 us
    ppermute x5, starting transfers between devices, from_behind(): return lax.ppermute(block, axis, route)  14.4 us
    dot_general x1, matrix products, body(): jnp.einsum('ihv,ihe->ive', blocks, row_entries, preferred_element_type=jn...  13.9 us
    gather x1, local copies, waits for them, and re-layouts, body(): column_entries = gathered[col_local]  13.6 us
  transfers between devices with their start and end apart: 6, of which 2 were waited for; matrix products, arithmetic and copies ran while one was open for 32% of the time, Pallas kernels for 0%

commit v1 on v0

--- a/solution.py
+++ b/solution.py
@@ -19,7 +19,15 @@
     my_row = lax.axis_index("row")
     segment = elem_dev * lax.axis_size("col")
     window = (REACH + 1) * elem_dev
-    row_group = lax.all_gather(coeffs, "col", axis=0, tiled=True)
+    x = coeffs
+    ways, here, step = (lax.axis_size("col"), lax.axis_index("col"), x.shape[0])
+    lengths = [n * ways if d == 0 else n for d, n in enumerate(x.shape)]
+    row_group = lax.dynamic_update_slice_in_dim(jnp.zeros(lengths, x.dtype), x, here * step, axis=0)
+    for far in range(1, ways):
+        x = lax.ppermute(x, "col", [(d, (d + 1) % ways) for d in range(ways)])
+        row_group = lax.dynamic_update_slice_in_dim(
+            row_group, x, (here - far) % ways * step, axis=0
+        )
     gathered = coeffs
     spread = 1
     for level in range(REACH.bit_length()):

time: 200 us -> 179 us (0.90)
  waiting for transfers between devices: 41.7 us -> 25.8 us
  blocking collectives: 13.1 us -> 0 us
  starting transfers between devices: 14.4 us -> 19.5 us
    unnamed x2, waiting for transfers between devices: 36.1 us -> 13.7 us
    all_gather x1 -> x0, blocking collectives: 13.1 us -> none  [body(): row_group = lax.all_gather(coeffs, 'col', axis=0, tiled=True)]
    ppermute x0 -> x3, starting transfers between devices: none -> 6.23 us  [body(): x = lax.ppermute(x, 'col', [(d, (d + 1) % ways) for d in range(ways)])]
    ppermute x0 -> x3, waiting for transfers between devices: none -> 5.61 us  [body(): x = lax.ppermute(x, 'col', [(d, (d + 1) % ways) for d in range(ways)])]
    unnamed x10 -> x6, local copies, waits for them, and re-layouts: 16.3 us -> 16.3 us
  transfers between devices with their start and end apart: 6 -> 9, of which waited for: 2 -> 4; matrix products, arithmetic and copies ran while one was open for 32% -> 38% of each run, Pallas kernels for 0% -> 0%
where the time goes in v1:
time: 179 us
  matrix products  70 us (39%)
  local copies, waits for them, and re-layouts  45.2 us (25%)
  waiting for transfers between devices  25.8 us (14%)
  starting transfers between devices  19.5 us (11%)
  between operations  14.9 us (8%)
  other arithmetic  3.2 us (2%)
    dot_general x1, matrix products, body(): jnp.dot(row_select, row_contributions, precision=high_precision, preferre...  21.2 us
    dot_general x1, matrix products, body(): jnp.dot(col_select, column_contributions, precision=high_precision, prefe...  20.6 us
    unnamed x6, local copies, waits for them, and re-layouts  16.3 us
    dot_general x1, matrix products, body(): jnp.einsum('gjc,gcx->gjx', blocks, column_entries, preferred_element_type...  14.4 us
    dot_general x1, matrix products, body(): jnp.einsum('ihv,ihe->ive', blocks, row_entries, preferred_element_type=jn...  13.8 us
    unnamed x2, waiting for transfers between devices  13.7 us
    gather x1, local copies, waits for them, and re-layouts, body(): column_entries = gathered[col_local]  13.5 us
    gather x1, local copies, waits for them, and re-layouts, body(): row_entries = row_group[row_local]  13.5 us
  transfers between devices with their start and end apart: 9, of which 4 were waited for; matrix products, arithmetic and copies ran while one was open for 38% of the time, Pallas kernels for 0%

profile of v1, /device:TPU:0, one launch (start us, length us, event | category | flops | bytes accessed | tf_op | source)
XLA Modules:
  0.0 178.5 jit_solution(15841369825017157357)
XLA Ops:
  6.5 3.0 %collective-permute-start.2 = (bf16[8,64,128]{2,1,0:T(8,128)(2,1)}, bf16[8,64,128]{2,1,0:T(8,128)(2,1)S(1)}, u32[]{:S(2)}, u32[]{:S(2)}) collective-permute-start(bf16[8,64,128]{2,1,0:T(8,128)(2,1)} %param.5), channel_id=1, source_target_pairs={{0,1},{1,2},{2,3},{3,0},{4,5},{5,6},{6,7},{7,4},{8,9},{9,10},{10,1... | collective-permute-start | bytes 393224 | tf_op jit(solution)/shard_map/ppermute | solution.py:27
  9.5 1.3 collective-permute-start
  10.8 0.7 compare_select_fusion.1
  12.2 0.7 compare_select_fusion
  12.8 0.7 compare_and_fusion
  13.5 0.1 broadcast_in_dim.7
  13.7 0.9 constant_dynamic-update-slice_fusion.3
  14.6 1.5 collective-permute-start.3
  16.2 15.7 %copy.10 = bf16[512,64,64]{1,2,0:T(8,128)(2,1)} copy(bf16[512,64,64]{0,2,1:T(8,128)(2,1)} %param.6) | data formatting | bytes 8388608 | tf_op args[1]
  31.9 1.3 collective-permute-start.1
  33.2 0.0 collective-permute-done.3
  33.2 1.7 collective-permute-start.4
  35.0 5.6 %collective-permute-done.4 = bf16[8,64,128]{2,1,0:T(8,128)(2,1)S(1)} collective-permute-done((bf16[8,64,128]{2,1,0:T(8,128)(2,1)S(1)}, bf16[8,64,128]{2,1,0:T(8,128)(2,1)S(1)}, u32[]{:S(2)}, u32[]{:S(2)}) %collective-permute-start.4) | collective-permute-done | bytes 131104 | tf_op jit(solution)/shard_map/ppermute | solution.py:27
  40.6 13.5 %gather_fusion.1 = bf16[512,64,128]{2,1,0:T(8,128)(2,1)} fusion(bf16[32,64,128]{2,1,0:T(8,128)(2,1)S(1)} %constant_dynamic-update-slice_fusion, s32[1024]{0:T(1024)S(1)} %pad_clamp_fusion), kind=kCustom, calls=%fused_computation.1 | custom fusion | bytes 16779264 | tf_op jit(solution)/shard_map/gather | solution.py:50
  54.1 13.8 %fusion.28 = f32[512,128,64]{1,2,0:T(8,128)} fusion(bf16[512,64,64]{1,2,0:T(8,128)(2,1)} %copy.10, bf16[512,64,128]{2,1,0:T(8,128)(2,1)} %gather_fusion.1), kind=kOutput, calls=%fused_computation.50 | convolution fusion | flops 536870912 | bytes 29360128 | tf_op jit(solution)/shard_map/ihv,ihe->ive/dot_general | solution.py:51
  67.9 0.1 pad_maximum_fusion
  67.9 13.5 %gather_fusion = bf16[512,64,128]{2,1,0:T(8,128)(2,1)} fusion(bf16[32,64,128]{2,1,0:T(8,128)(2,1)S(1)} %pad_maximum_fusion, s32[1024]{0:T(1024)S(1)} %pad_clamp_fusion.1), kind=kCustom, calls=%fused_computation | custom fusion | bytes 16779264 | tf_op jit(solution)/shard_map/gather | solution.py:42
  81.5 14.4 %fusion.27 = f32[512,128,64]{1,2,0:T(8,128)} fusion(bf16[512,64,64]{1,2,0:T(8,128)(2,1)} %copy.10, bf16[512,64,128]{2,1,0:T(8,128)(2,1)} %gather_fusion), kind=kOutput, calls=%fused_computation.49 | convolution fusion | flops 536870912 | bytes 29360128 | tf_op jit(solution)/shard_map/gjc,gcx->gjx/dot_general | solution.py:43
  95.9 21.2 %fusion.3 = f32[32,8192]{1,0:T(8,128)} fusion(f32[64,8,64,128]{3,2,1,0:T(8,128)} %bitcast.21, s32[512]{0:T(512)S(1)} %get-tuple-element.8, pred[512]{0:T(512)(128)(4,1)S(1)} %iota_compare_fusion.2), kind=kOutput, calls=%fused_computation.5 | convolution fusion | flops 1610645504 | bytes 17828352 | tf_op jit(solution)/shard_map/dot_general | solution.py:64
  117.1 0.0 all-reduce.3.cloned.1.call-update
  117.1 0.0 copy-start.1
  117.1 20.6 %fusion = f32[32,8192]{1,0:T(8,128)S(1)} fusion(f32[64,8,64,128]{3,2,1,0:T(8,128)} %bitcast.20, s32[512]{0:T(512)S(1)} %get-tuple-element.6, pred[512]{0:T(512)(128)(4,1)S(1)} %compare_and_fusion), kind=kOutput, calls=%fused_computation.2 | convolution fusion | flops 1610645504 | bytes 17828352 | tf_op jit(solution)/shard_map/dot_general | solution.py:58
  137.7 0.1 fusion.26
  137.8 1.9 %collective-permute-start.5 = (f32[8,8192]{1,0:T(8,128)S(1)}, f32[8,8192]{1,0:T(8,128)S(1)}, u32[]{:S(2)}, u32[]{:S(2)}) collective-permute-start(f32[8,8192]{1,0:T(8,128)S(1)} %get-tuple-element.9), channel_id=1, source_target_pairs={{0,4},{4,8},{8,12},{12,16},{16,20},{20,24},{24,28},{1,5},{5,9},{9,... | collective-permute-start | bytes 786440 | tf_op jit(solution)/shard_map/ppermute | solution.py:12
  139.7 4.3 %collective-permute-start.6 = (f32[8,8192]{1,0:T(8,128)S(1)}, f32[8,8192]{1,0:T(8,128)S(1)}, u32[]{:S(2)}, u32[]{:S(2)}) collective-permute-start(f32[8,8192]{1,0:T(8,128)S(1)} %get-tuple-element.11), channel_id=1, source_target_pairs={{0,8},{4,12},{8,16},{12,20},{16,24},{20,28},{1,9},{5,13},{9,17},{1... | collective-permute-start | bytes 786440 | tf_op jit(solution)/shard_map/ppermute | solution.py:12
  144.0 4.5 %collective-permute-start.7 = (f32[8,8192]{1,0:T(8,128)S(1)}, f32[8,8192]{1,0:T(8,128)S(1)}, u32[]{:S(2)}, u32[]{:S(2)}) collective-permute-start(f32[8,8192]{1,0:T(8,128)S(1)} %get-tuple-element.10), channel_id=1, source_target_pairs={{0,12},{4,16},{8,20},{12,24},{16,28},{1,13},{5,17},{9,21},{13,25},... | collective-permute-start | bytes 786440 | tf_op jit(solution)/shard_map/ppermute | solution.py:12
  148.5 0.6 dynamic-slice
  149.8 0.9 collective-permute-done.6
  150.6 5.6 %collective-permute-done.7 = f32[8,8192]{1,0:T(8,128)S(1)} collective-permute-done((f32[8,8192]{1,0:T(8,128)S(1)}, f32[8,8192]{1,0:T(8,128)S(1)}, u32[]{:S(2)}, u32[]{:S(2)}) %collective-permute-start.7) | collective-permute-done | bytes 262176 | tf_op jit(solution)/shard_map/ppermute | solution.py:12
  156.2 13.7 %all-reduce.3.cloned.1.call-done = f32[32,8192]{1,0:T(8,128)} async-done(((f32[32,8192]{1,0:T(8,128)}), f32[32,8192]{1,0:T(8,128)}) %all-reduce.3.cloned.1.call-update) | async-done | bytes 1048592
  169.9 1.0 fusion.9
  170.9 0.8 copy.11
  (15 shorter events, 0.1 us)
Async XLA Ops:
  6.5 25.3 %copy-start = (bf16[8,64,128]{2,1,0:T(8,128)(2,1)S(1)}, bf16[8,64,128]{2,1,0:T(8,128)(2,1)}, u32[]{:S(2)}) copy-start(bf16[8,64,128]{2,1,0:T(8,128)(2,1)} %param.5) | copy-start | bytes 393220
  6.5 163.4 %all-reduce.3.cloned.1.call-start = ((), (), s32[]{:S(2)}) async-start(), calls=%async_computation | async-start | bytes 2097152
  6.5 8.1 %collective-permute-start.2 = (bf16[8,64,128]{2,1,0:T(8,128)(2,1)}, bf16[8,64,128]{2,1,0:T(8,128)(2,1)S(1)}, u32[]{:S(2)}, u32[]{:S(2)}) collective-permute-start(bf16[8,64,128]{2,1,0:T(8,128)(2,1)} %param.5), channel_id=1, source_target_pairs={{0,1},{1,2},{2,3},{3,0},{4,5},{5,6},{6,7},{7,4},{8,9},{9,10},{10,1... | collective-permute-start | bytes 393224 | tf_op jit(solution)/shard_map/ppermute | solution.py:27
  9.5 22.3 %collective-permute-start = (bf16[8,64,128]{2,1,0:T(8,128)(2,1)}, bf16[8,64,128]{2,1,0:T(8,128)(2,1)S(1)}, u32[]{:S(2)}, u32[]{:S(2)}) collective-permute-start(bf16[8,64,128]{2,1,0:T(8,128)(2,1)} %param.5), channel_id=1, source_target_pairs={{4,0},{8,4},{12,8},{16,12},{20,16},{24,20},{28,24},{5,1},{9,5},{13... | collective-permute-start | bytes 393224 | tf_op jit(solution)/shard_map/ppermute | solution.py:12
  14.6 18.5 %collective-permute-start.3 = (bf16[8,64,128]{2,1,0:T(8,128)(2,1)S(1)}, bf16[8,64,128]{2,1,0:T(8,128)(2,1)S(1)}, u32[]{:S(2)}, u32[]{:S(2)}) collective-permute-start(bf16[8,64,128]{2,1,0:T(8,128)(2,1)S(1)} %collective-permute-done.2), channel_id=1, source_target_pairs={{0,1},{1,2},{2,3},{3,0},{4,5},{5,6},{6,7},{7,4},{8,9},{9,10},{10,1... | collective-permute-start | bytes 393224 | tf_op jit(solution)/shard_map/ppermute | solution.py:27
  31.9 36.0 %collective-permute-start.1 = (bf16[16,64,128]{2,1,0:T(8,128)(2,1)S(1)}, bf16[16,64,128]{2,1,0:T(8,128)(2,1)S(1)}, u32[]{:S(2)}, u32[]{:S(2)}) collective-permute-start(bf16[16,64,128]{2,1,0:T(8,128)(2,1)S(1)} %pad_maximum_fusion.1), channel_id=1, source_target_pairs={{8,0},{12,4},{16,8},{20,12},{24,16},{28,20},{9,1},{13,5},{17,9},{2... | collective-permute-start | bytes 786440 | tf_op jit(solution)/shard_map/ppermute | solution.py:12
  33.2 7.4 %collective-permute-start.4 = (bf16[8,64,128]{2,1,0:T(8,128)(2,1)S(1)}, bf16[8,64,128]{2,1,0:T(8,128)(2,1)S(1)}, u32[]{:S(2)}, u32[]{:S(2)}) collective-permute-start(bf16[8,64,128]{2,1,0:T(8,128)(2,1)S(1)} %collective-permute-done.3), channel_id=1, source_target_pairs={{0,1},{1,2},{2,3},{3,0},{4,5},{5,6},{6,7},{7,4},{8,9},{9,10},{10,1... | collective-permute-start | bytes 393224 | tf_op jit(solution)/shard_map/ppermute | solution.py:27
  117.1 31.4 %copy-start.1 = (u32[32]{0:T(128)S(1)}, u32[32]{0:T(128)}, u32[]{:S(2)}) copy-start(u32[32]{0:T(128)} %constant.79) | copy-start | bytes 388
  137.8 12.0 %collective-permute-start.5 = (f32[8,8192]{1,0:T(8,128)S(1)}, f32[8,8192]{1,0:T(8,128)S(1)}, u32[]{:S(2)}, u32[]{:S(2)}) collective-permute-start(f32[8,8192]{1,0:T(8,128)S(1)} %get-tuple-element.9), channel_id=1, source_target_pairs={{0,4},{4,8},{8,12},{12,16},{16,20},{20,24},{24,28},{1,5},{5,9},{9,... | collective-permute-start | bytes 786440 | tf_op jit(solution)/shard_map/ppermute | solution.py:12
  139.7 10.9 %collective-permute-start.6 = (f32[8,8192]{1,0:T(8,128)S(1)}, f32[8,8192]{1,0:T(8,128)S(1)}, u32[]{:S(2)}, u32[]{:S(2)}) collective-permute-start(f32[8,8192]{1,0:T(8,128)S(1)} %get-tuple-element.11), channel_id=1, source_target_pairs={{0,8},{4,12},{8,16},{12,20},{16,24},{20,28},{1,9},{5,13},{9,17},{1... | collective-permute-start | bytes 786440 | tf_op jit(solution)/shard_map/ppermute | solution.py:12
  144.0 12.2 %collective-permute-start.7 = (f32[8,8192]{1,0:T(8,128)S(1)}, f32[8,8192]{1,0:T(8,128)S(1)}, u32[]{:S(2)}, u32[]{:S(2)}) collective-permute-start(f32[8,8192]{1,0:T(8,128)S(1)} %get-tuple-element.10), channel_id=1, source_target_pairs={{0,12},{4,16},{8,20},{12,24},{16,28},{1,13},{5,17},{9,21},{13,25},... | collective-permute-start | bytes 786440 | tf_op jit(solution)/shard_map/ppermute | solution.py:12
Sparse Core Ops, SparseCore 0:
  117.2 52.6 all-reduce.2
